TPU v7x, 32 devices: a whole 2x2x4 slice. The times are simulated.
32 devices in a mesh: groups: 2 (over x), gx: 16 (over z, y, core).
Axes of the slice: x: 2, y: 2, z: 4, core: 2. Of those that a mesh axis runs over, the one named last changes fastest.
Arguments:
- features: bfloat16 [64, 16, 64, 128], P(('groups', 'gx')), parts along dimension 0, may hold values from -6 to 6
- cotangent: bfloat16 [64, 16, 64, 128], P(('groups', 'gx')), parts along dimension 0, may hold values from -6 to 6
- wall_flags: int32 [64, 16, 128], P(('groups', 'gx')), parts along dimension 0, may hold values 0 or 1
- mode_counts: int32 [64], replicated, may hold values from 1 to 16, as said below
- offsets: int32 [6, 3], replicated, may hold values from -2 to 2, as said below
- point_weight: bfloat16 [64, 64], replicated, may hold values from -0.75 to 0.75
- kernel_weight: bfloat16 [6, 64, 64], replicated, may hold values from -0.3125 to 0.3125
- lap_weight: bfloat16 [64, 64], replicated, may hold values from -0.125 to 0.125
- spec_weight: bfloat16 [16, 64, 64], replicated, may hold values from -1 to 1
- bias: float32 [64], replicated, may hold values from -3 to 3
Outputs:
- input_grad: bfloat16 [64, 16, 64, 128], P(('groups', 'gx')), parts along dimension 0
- kernel_grad: float32 [12, 64, 64], P('groups'), parts along dimension 0
There are 2 independent parts, one for each index of `groups`. A program takes and returns all parts, laid end to end along the dimension named above; an argument that names none is the same for every part. Nothing has to cross between parts.
Inputs may be any that keep to these rules, and one draw needn't show every extreme that they name: Column 0 holds x offsets in -1..1 and both -1 and 1 occur; columns 1 and 2 hold y and z offsets in -2..2, and -2 and 2 occur in each of them. `mode_counts`: some channel keeps 16 modes and some channel keeps 1.
All inputs are finite; a program needn't handle non-finite values. No bound on the sum of `wall_flags` on one device may be relied on, other than what follows from the above.
Results may differ from a plain program's by a relative error of at most 0.0066.
Values may be sent and summed in bfloat16 or wider, within the bound.
A program may use at most 256 MiB of HBM per device.

v0:
```python
from functools import partial
import math

import jax
import jax.numpy as jnp
from jax import lax
from jax.sharding import PartitionSpec as P

RAD = 2


def with_halo(cells, sides, width):
    for axis, dim in sides:
        count = lax.axis_size(axis)
        ends = count - 1
        head = lax.slice_in_dim(cells, 0, width, axis=dim)
        tail = lax.slice_in_dim(cells, cells.shape[dim] - width, cells.shape[dim], axis=dim)
        cells = jnp.concatenate(
            [
                lax.ppermute(tail, axis, [(i, (i + 1) % count) for i in range(ends)]),
                cells,
                lax.ppermute(head, axis, [((i + 1) % count, i) for i in range(ends)]),
            ],
            axis=dim,
        )
    return cells


def basis_table(mode_total, length):
    mode_index = jnp.arange(mode_total, dtype=jnp.float32)[:, None]
    cell_index = jnp.arange(length, dtype=jnp.float32)[None, :]
    phase_angle = math.pi / (2.0 * length) * mode_index * (2.0 * cell_index + 1.0)
    amplitude = jnp.where(mode_index == 0.0, math.sqrt(1.0 / length), math.sqrt(2.0 / length))
    return (amplitude * jnp.cos(phase_angle)).astype(jnp.bfloat16)


def pencil_work(pencil, spec_weight, kept_modes, adjoint):
    basis = basis_table(spec_weight.shape[0], pencil.shape[0])
    coefficients = jnp.einsum(
        "kx,xycz->kycz", basis, pencil, preferred_element_type=jnp.float32
    ).astype(jnp.bfloat16)
    if adjoint:
        masked = coefficients * kept_modes[:, None, :, None].astype(jnp.bfloat16)
        mixed_modes = jnp.einsum(
            "koc,kyoz->kycz", spec_weight, masked, preferred_element_type=jnp.float32
        ).astype(jnp.bfloat16)
    else:
        mixed_modes = jnp.einsum(
            "koc,kycz->kyoz", spec_weight, coefficients, preferred_element_type=jnp.float32
        )
        mixed_modes = (mixed_modes * kept_modes[:, None, :, None]).astype(jnp.bfloat16)
    return jnp.einsum(
        "kx,kyoz->xyoz", basis, mixed_modes, preferred_element_type=jnp.float32
    ).astype(jnp.bfloat16)


def spectral(slab, spec_weight, kept_modes, adjoint):
    result = pencil_work(
        lax.all_to_all(slab, "gx", split_axis=1, concat_axis=0, tiled=True),
        spec_weight,
        kept_modes,
        adjoint,
    )
    return lax.all_to_all(result, "gx", split_axis=0, concat_axis=1, tiled=True)


def laplace_ext(extended):
    padded = jnp.pad(extended, ((0, 0), (1, 1), (0, 0), (1, 1))).astype(jnp.float32)
    centre_cells = padded[1:-1, 1:-1, :, 1:-1]
    neighbours = padded[2:, 1:-1, :, 1:-1] + padded[:-2, 1:-1, :, 1:-1]
    neighbours = neighbours + padded[1:-1, 2:, :, 1:-1] + padded[1:-1, :-2, :, 1:-1]
    neighbours = neighbours + padded[1:-1, 1:-1, :, 2:] + padded[1:-1, 1:-1, :, :-2]
    return (neighbours - 6.0 * centre_cells).astype(jnp.bfloat16)


def pad_sides(extended):
    return jnp.pad(extended, ((0, 0), (RAD, RAD), (0, 0), (RAD, RAD)))


def window_of(padded, offset, direction, slab_shape):
    starts = (
        1 + direction * offset[0],
        RAD + direction * offset[1],
        0,
        RAD + direction * offset[2],
    )
    return lax.dynamic_slice(padded, starts, slab_shape)


def gelu_slope(preact, upstream):
    _, pullback = jax.vjp(partial(jax.nn.gelu, approximate=True), preact)
    return pullback(upstream)[0]


def per_device(
    features,
    cotangent,
    wall_flags,
    mode_counts,
    offsets,
    point_weight,
    kernel_weight,
    lap_weight,
    spec_weight,
    bias,
):
    mode_total = spec_weight.shape[0]
    tile_total = kernel_weight.shape[0]
    kept_modes = (jnp.arange(mode_total, dtype=jnp.int32)[:, None] < mode_counts[None, :]).astype(
        jnp.float32
    )
    fluid_mask = (1 - wall_flags).astype(jnp.float32)[:, :, None, :]
    extended = with_halo(features, (("gx", 0),), 1)
    padded_field = pad_sides(extended)
    local_part = jnp.einsum(
        "oc,xycz->xyoz", point_weight, features, preferred_element_type=jnp.float32
    )
    local_part = local_part + jnp.einsum(
        "oc,xycz->xyoz", lap_weight, laplace_ext(extended), preferred_element_type=jnp.float32
    )
    for tile in range(tile_total):
        moved = window_of(padded_field, offsets[tile], 1, features.shape)
        local_part = local_part + jnp.einsum(
            "oc,xycz->xyoz", kernel_weight[tile], moved, preferred_element_type=jnp.float32
        )
    local_part = local_part + bias[:, None]
    spectral_part = spectral(features, spec_weight, kept_modes, False)
    preact = local_part + spectral_part.astype(jnp.float32)
    weighted = (gelu_slope(preact, cotangent.astype(jnp.float32)) * fluid_mask).astype(jnp.bfloat16)
    spec_grad = spectral(weighted, spec_weight, kept_modes, True)
    ext_grad = with_halo(weighted, (("gx", 0),), 1)
    padded_grad = pad_sides(ext_grad)
    input_grad = jnp.einsum(
        "oc,xyoz->xycz", point_weight, weighted, preferred_element_type=jnp.float32
    )
    input_grad = input_grad + jnp.einsum(
        "oc,xyoz->xycz", lap_weight, laplace_ext(ext_grad), preferred_element_type=jnp.float32
    )
    input_grad = input_grad + spec_grad.astype(jnp.float32)
    tile_grads = []
    for tile in range(tile_total):
        back_moved = window_of(padded_grad, offsets[tile], -1, weighted.shape)
        input_grad = input_grad + jnp.einsum(
            "oc,xyoz->xycz", kernel_weight[tile], back_moved, preferred_element_type=jnp.float32
        )
        tile_grads.append(
            jnp.einsum("xyoz,xycz->oc", back_moved, features, preferred_element_type=jnp.float32)
        )
    local_grad = jnp.stack(tile_grads, axis=0)
    scaling = float(
        lax.axis_size("gx") * features.shape[0] * features.shape[1] * features.shape[3]
    ) ** (-0.5)
    summed = lax.psum(local_grad, "gx")
    return (input_grad.astype(jnp.bfloat16), summed * scaling)


def solution(mesh):
    return jax.shard_map(
        per_device,
        mesh=mesh,
        in_specs=(
            P(("groups", "gx"), None, None, None),
            P(("groups", "gx"), None, None, None),
            P(("groups", "gx"), None, None),
            P(),
            P(),
            P(),
            P(),
            P(),
            P(),
            P(),
        ),
        out_specs=(P(("groups", "gx"), None, None, None), P("groups", None, None)),
        check_vma=False,
    )
```

profile of v0, /device:TPU:0, one launch (start us, length us, event | category | flops | bytes accessed | tf_op | source)
XLA Modules:
  0.0 241.2 jit_solution(13705008029308537028)
XLA Ops:
  7.2 1.1 fusion.148
  8.4 2.4 collective-permute-start
  10.7 1.3 collective-permute-start.1
  12.0 1.9 copy.40
  13.9 9.4 %all-to-all-start = ((bf16[2,16,64,128]{3,2,0,1:T(8,128)(2,1)}), bf16[2,16,64,128]{3,2,0,1:T(8,128)(2,1)S(1)}, u32[]{:S(2)}, u32[]{:S(2)}) async-start(bf16[2,16,64,128]{3,2,0,1:T(8,128)(2,1)} %copy.40), calls=%async_computation | async-start | bytes 1048576 | tf_op jit(solution)/shard_map/all_to_all | solution.py:59
  23.4 1.3 fusion.76
  61.1 1.5 fusion.48
  62.6 1.4 fusion.49
  64.0 1.1 convolution_convert_fusion.4
  65.3 1.1 fusion.17
  67.4 6.0 %all-to-all-start.1 = ((bf16[32,1,64,128]{3,2,1,0:T(8,128)(2,1)}), bf16[32,1,64,128]{3,2,1,0:T(8,128)(2,1)S(1)}, u32[]{:S(2)}, u32[]{:S(2)}) async-start(bf16[32,1,64,128]{3,2,1,0:T(8,128)(2,1)} %copy.44), calls=%async_computation.1 | async-start | bytes 1048576 | tf_op jit(solution)/shard_map/all_to_all | solution.py:64
  74.2 1.4 fusion.50
  75.7 1.4 fusion.51
  77.1 2.9 %convolution_add_fusion.1 = f32[2,16,128,64]{2,3,1,0:T(8,128)} fusion(f32[2,16,128,64]{2,3,1,0:T(8,128)S(1)} %copy-done.3, f32[4,18,64,130]{3,2,1,0:T(8,128)S(1)} %pad_convert_fusion.1, bf16[64,64]{1,0:T(8,128)(2,1)S(1)} %copy-done.12), kind=kOutput, calls=%fused_computation.37 | convolution fusion | flops 35913728 | bytes 9453568 | tf_op jit(solution)/shard_map/oc,xycz->xyoz/dot_general | solution.py:118
  79.9 8.0 %all-to-all-done.1 = bf16[32,1,64,128]{3,2,1,0:T(8,128)(2,1)S(1)} async-done(((bf16[32,1,64,128]{3,2,1,0:T(8,128)(2,1)}), bf16[32,1,64,128]{3,2,1,0:T(8,128)(2,1)S(1)}, u32[]{:S(2)}, u32[]{:S(2)}) %all-to-all-start.1) | async-done | bytes 524320 | tf_op jit(solution)/shard_map/all_to_all | solution.py:64
  88.7 4.2 %fusion.33 = bf16[2,16,64,128]{3,2,1,0:T(8,128)(2,1)S(1)} fusion(bf16[2,16,64,128]{3,2,1,0:T(8,128)(2,1)} %param.11, f32[2,16,128,64]{2,3,1,0:T(8,128)} %fusion.51, f32[2,16,128,64]{2,3,1,0:T(8,128)} %fusion.50, f32[2,16,128,64]{2,3,1,0:T(8,128)} %fusion.49, f32[2,16,128,64]{2,3,1,0:T(8,128)} %fusion.48, f32[2,16,128,64]{2,3,1,0:T(8,128)S(1)} %fusion.47, ...), kind=kOutput, calls=%fused_computation.72 | convolution fusion | flops 41680896 | bytes 8946188 | tf_op jit(solution)/shard_map/oc,xycz->xyoz/dot_general | solution.py:123
  93.7 1.9 collective-permute-start.2
  95.7 1.3 collective-permute-start.3
  97.0 6.9 %all-to-all-start.2 = ((bf16[2,16,64,128]{3,2,0,1:T(8,128)(2,1)}), bf16[2,16,64,128]{3,2,0,1:T(8,128)(2,1)}, u32[]{:S(2)}, u32[]{:S(2)}) async-start(bf16[2,16,64,128]{3,2,0,1:T(8,128)(2,1)} %copy.49), calls=%async_computation.2 | async-start | bytes 1048576 | tf_op jit(solution)/shard_map/all_to_all | solution.py:59
  103.9 1.3 fusion.74
  110.9 1.5 convolution_bitcast_fusion.2
  112.3 1.4 convolution_bitcast_fusion.3
  113.7 4.7 %all-to-all-done.2 = bf16[2,16,64,128]{3,2,0,1:T(8,128)(2,1)} async-done(((bf16[2,16,64,128]{3,2,0,1:T(8,128)(2,1)}), bf16[2,16,64,128]{3,2,0,1:T(8,128)(2,1)}, u32[]{:S(2)}, u32[]{:S(2)}) %all-to-all-start.2) | async-done | bytes 524320 | tf_op jit(solution)/shard_map/all_to_all | solution.py:59
  118.4 1.5 fusion.22
  121.7 4.1 %all-to-all-start.3 = ((bf16[32,1,64,128]{3,2,1,0:T(8,128)(2,1)}), bf16[32,1,64,128]{3,2,1,0:T(8,128)(2,1)S(1)}, u32[]{:S(2)}, u32[]{:S(2)}) async-start(bf16[32,1,64,128]{3,2,1,0:T(8,128)(2,1)} %copy.55), calls=%async_computation.3 | async-start | bytes 1048576 | tf_op jit(solution)/shard_map/all_to_all | solution.py:64
  126.9 1.4 convolution_bitcast_fusion.4
  128.3 1.5 convolution_bitcast_fusion
  129.8 2.9 %pad_convert_fusion = f32[4,18,64,130]{3,2,1,0:T(8,128)} fusion(bf16[4,16,64,128]{3,2,1,0:T(8,128)(2,1)S(1)} %pad_maximum_fusion), kind=kLoop, calls=%fused_computation.12 | loop fusion | flops 599040 | bytes 3444736 | tf_op jit(solution)/shard_map/convert_element_type | solution.py:68
  132.7 89.0 %all-reduce.6.cloned.1.call-done = f32[6,64,64]{2,1,0:T(8,128)} async-done(((f32[6,64,64]{2,1,0:T(8,128)}), f32[6,64,64]{2,1,0:T(8,128)}) %all-reduce.6.cloned.1.call-update) | async-done | bytes 98320 | tf_op jit(solution)/shard_map/psum | solution.py:153
  221.7 1.6 broadcast_multiply_fusion
  223.4 7.5 %fusion.15 = f32[2,16,64,128]{3,2,1,0:T(8,128)S(1)} fusion(f32[2,16,128,64]{2,3,1,0:T(8,128)} %fusion.74, f32[4,18,64,130]{3,2,1,0:T(8,128)} %pad_convert_fusion, bf16[64,64]{1,0:T(8,128)(2,1)S(1)} %copy-done.13, bf16[16,2,1,64,128]{4,3,1,0,2:T(8,128)(2,1)S(1)} %bitcast.306), kind=kOutput, calls=%fused_computation.40 | convolution fusion | flops 36438016 | bytes 9969664 | tf_op jit(solution)/shard_map/oc,xyoz->xycz/dot_general | solution.py:136
  230.8 3.5 %fusion.16 = bf16[2,16,64,128]{3,2,1,0:T(8,128)(2,1)} fusion(f32[2,16,64,128]{3,2,1,0:T(8,128)} %convolution_bitcast_fusion, f32[2,16,64,128]{3,2,1,0:T(8,128)S(1)} %convolution_bitcast_fusion.1, f32[2,16,64,128]{3,2,1,0:T(8,128)} %convolution_bitcast_fusion.2, f32[2,16,64,128]{3,2,1,0:T(8,128)} %convolution_bitcast_fusion.3, ...), kind=kOutput, calls=%fused_computation.43 | convolution fusion | flops 35389440 | bytes 7880716 | tf_op jit(solution)/shard_map/oc,xyoz->xycz/dot_general | solution.py:143
  (62 shorter events, 14.6 us)
Async XLA Ops:
  7.2 57.9 %copy-start = (bf16[16,64,64]{2,1,0:T(8,128)(2,1)S(1)}, bf16[16,64,64]{2,1,0:T(8,128)(2,1)}, u32[]{:S(2)}) copy-start(bf16[16,64,64]{2,1,0:T(8,128)(2,1)} %param.18) | copy-start | bytes 393220
  7.2 16.2 %copy-start.1 = (bf16[2,16,64,128]{3,2,1,0:T(8,128)(2,1)S(1)}, bf16[2,16,64,128]{3,2,1,0:T(8,128)(2,1)}, u32[]{:S(2)}) copy-start(bf16[2,16,64,128]{3,2,1,0:T(8,128)(2,1)} %param.10) | copy-start | bytes 1572868
  7.2 16.2 %copy-start.11 = (s32[64]{0:T(128)S(1)}, s32[64]{0:T(128)}, u32[]{:S(2)}) copy-start(s32[64]{0:T(128)} %param.13) | copy-start | bytes 772
  7.2 16.2 %copy-start.5 = (bf16[64,64]{1,0:T(8,128)(2,1)S(1)}, bf16[64,64]{1,0:T(8,128)(2,1)}, u32[]{:S(2)}) copy-start(bf16[64,64]{1,0:T(8,128)(2,1)} %param.15) | copy-start | bytes 24580
  7.2 17.5 %copy-start.8 = (s32[2,16,128]{2,1,0:T(8,128)S(1)}, s32[2,16,128]{2,1,0:T(8,128)}, u32[]{:S(2)}) copy-start(s32[2,16,128]{2,1,0:T(8,128)} %param.12) | copy-start | bytes 49156
  7.2 17.5 %copy-start.6 = (s32[6,3]{0,1:T(4,128)S(1)}, s32[6,3]{0,1:T(4,128)}, u32[]{:S(2)}) copy-start(s32[6,3]{0,1:T(4,128)} %param.14) | copy-start | bytes 220
  8.4 52.2 %collective-permute-start = (bf16[1,16,64,128]{3,2,1,0:T(8,128)(2,1)S(1)}, bf16[1,16,64,128]{3,2,1,0:T(8,128)(2,1)S(1)}, u32[]{:S(2)}, u32[]{:S(2)}) collective-permute-start(bf16[1,16,64,128]{3,2,1,0:T(8,128)(2,1)S(1)} %get-tuple-element.5), channel_id=1, source_target_pairs={{0,1},{1,2},{2,3},{3,4},{4,5},{5,6},{6,7},{7,8},{8,9},{9,10},{10,1... | collective-permute-start | bytes 786440 | tf_op jit(solution)/shard_map/ppermute | solution.py:20
  10.7 49.9 %collective-permute-start.1 = (bf16[1,16,64,128]{3,2,1,0:T(8,128)(2,1)S(1)}, bf16[1,16,64,128]{3,2,1,0:T(8,128)(2,1)S(1)}, u32[]{:S(2)}, u32[]{:S(2)}) collective-permute-start(bf16[1,16,64,128]{3,2,1,0:T(8,128)(2,1)S(1)} %get-tuple-element.4), channel_id=1, source_target_pairs={{1,0},{2,1},{3,2},{4,3},{5,4},{6,5},{7,6},{8,7},{9,8},{10,9},{11,1... | collective-permute-start | bytes 786440 | tf_op jit(solution)/shard_map/ppermute | solution.py:22
  13.9 46.8 %copy-start.4 = (bf16[6,64,64]{2,1,0:T(8,128)(2,1)S(1)}, bf16[6,64,64]{2,1,0:T(8,128)(2,1)}, u32[]{:S(2)}) copy-start(bf16[6,64,64]{2,1,0:T(8,128)(2,1)} %param.16) | copy-start | bytes 147460
  13.9 50.1 %all-to-all-start = ((bf16[2,16,64,128]{3,2,0,1:T(8,128)(2,1)}), bf16[2,16,64,128]{3,2,0,1:T(8,128)(2,1)S(1)}, u32[]{:S(2)}, u32[]{:S(2)}) async-start(bf16[2,16,64,128]{3,2,0,1:T(8,128)(2,1)} %copy.40), calls=%async_computation | async-start | bytes 1048576 | tf_op jit(solution)/shard_map/all_to_all | solution.py:59
  67.4 20.5 %all-to-all-start.1 = ((bf16[32,1,64,128]{3,2,1,0:T(8,128)(2,1)}), bf16[32,1,64,128]{3,2,1,0:T(8,128)(2,1)S(1)}, u32[]{:S(2)}, u32[]{:S(2)}) async-start(bf16[32,1,64,128]{3,2,1,0:T(8,128)(2,1)} %copy.44), calls=%async_computation.1 | async-start | bytes 1048576 | tf_op jit(solution)/shard_map/all_to_all | solution.py:64
  74.2 2.9 %copy-start.3 = (f32[2,16,128,64]{2,3,1,0:T(8,128)S(1)}, f32[2,16,128,64]{2,3,1,0:T(8,128)}, u32[]{:S(2)}) copy-start(f32[2,16,128,64]{2,3,1,0:T(8,128)} %fusion.76) | copy-start | bytes 3145732
  74.2 2.9 %copy-start.12 = (bf16[64,64]{1,0:T(8,128)(2,1)S(1)}, bf16[64,64]{1,0:T(8,128)(2,1)}, u32[]{:S(2)}) copy-start(bf16[64,64]{1,0:T(8,128)(2,1)} %param.17) | copy-start | bytes 24580
  75.7 13.0 %copy-start.10 = (f32[64]{0:T(128)S(1)}, f32[64]{0:T(128)}, u32[]{:S(2)}) copy-start(f32[64]{0:T(128)} %param.19) | copy-start | bytes 772
  87.9 0.8 copy-start.2
  93.7 11.5 %collective-permute-start.2 = (bf16[1,16,64,128]{3,2,1,0:T(8,128)(2,1)S(1)}, bf16[1,16,64,128]{3,2,1,0:T(8,128)(2,1)S(1)}, u32[]{:S(2)}, u32[]{:S(2)}) collective-permute-start(bf16[1,16,64,128]{3,2,1,0:T(8,128)(2,1)S(1)} %get-tuple-element.2), channel_id=1, source_target_pairs={{0,1},{1,2},{2,3},{3,4},{4,5},{5,6},{6,7},{7,8},{8,9},{9,10},{10,1... | collective-permute-start | bytes 786440 | tf_op jit(solution)/shard_map/ppermute | solution.py:20
  95.7 9.6 %collective-permute-start.3 = (bf16[1,16,64,128]{3,2,1,0:T(8,128)(2,1)S(1)}, bf16[1,16,64,128]{3,2,1,0:T(8,128)(2,1)S(1)}, u32[]{:S(2)}, u32[]{:S(2)}) collective-permute-start(bf16[1,16,64,128]{3,2,1,0:T(8,128)(2,1)S(1)} %get-tuple-element.3), channel_id=1, source_target_pairs={{1,0},{2,1},{3,2},{4,3},{5,4},{6,5},{7,6},{8,7},{9,8},{10,9},{11,1... | collective-permute-start | bytes 786440 | tf_op jit(solution)/shard_map/ppermute | solution.py:22
  97.0 21.5 %all-to-all-start.2 = ((bf16[2,16,64,128]{3,2,0,1:T(8,128)(2,1)}), bf16[2,16,64,128]{3,2,0,1:T(8,128)(2,1)}, u32[]{:S(2)}, u32[]{:S(2)}) async-start(bf16[2,16,64,128]{3,2,0,1:T(8,128)(2,1)} %copy.49), calls=%async_computation.2 | async-start | bytes 1048576 | tf_op jit(solution)/shard_map/all_to_all | solution.py:59
  110.8 7.6 %copy-start.7 = (bf16[16,64]{0,1:T(8,128)(2,1)S(1)}, bf16[16,64]{0,1:T(8,128)(2,1)}, u32[]{:S(2)}) copy-start(bf16[16,64]{0,1:T(8,128)(2,1)} %copy.51) | copy-start | bytes 6148
  110.8 7.6 %copy-start.9 = (f32[32]{0:T(128)S(1)}, f32[32]{0:T(128)}, u32[]{:S(2)}) copy-start(f32[32]{0:T(128)} %multiply_add_fusion) | copy-start | bytes 388
  121.7 101.7 %all-to-all-start.3 = ((bf16[32,1,64,128]{3,2,1,0:T(8,128)(2,1)}), bf16[32,1,64,128]{3,2,1,0:T(8,128)(2,1)S(1)}, u32[]{:S(2)}, u32[]{:S(2)}) async-start(bf16[32,1,64,128]{3,2,1,0:T(8,128)(2,1)} %copy.55), calls=%async_computation.3 | async-start | bytes 1048576 | tf_op jit(solution)/shard_map/all_to_all | solution.py:64
  125.8 95.9 %all-reduce.6.cloned.1.call-start = ((), (), s32[]{:S(2)}) async-start(), calls=%async_computation.4 | async-start | bytes 393216 | tf_op jit(solution)/shard_map/psum | solution.py:153
  129.8 93.6 %copy-start.13 = (bf16[64,64]{1,0:T(8,128)(2,1)S(1)}, bf16[64,64]{1,0:T(8,128)(2,1)}, u32[]{:S(2)}) copy-start(bf16[64,64]{1,0:T(8,128)(2,1)} %param.17) | copy-start | bytes 24580
Sparse Core Ops, SparseCore 0:
  130.6 91.0 all-reduce.5
where the time goes:
time: 242 us; the launch traced here: 241 us
  waiting for transfers between devices  102 us (42%)
  between operations  48.2 us (20%)
  matrix products  43.7 us (18%)
  starting transfers between devices  33.4 us (14%)
  local copies, waits for them, and re-layouts  8.26 us (3%)
  other arithmetic  5.98 us (2%)
    psum x1, waiting for transfers between devices, per_device(): summed = lax.psum(local_grad, 'gx')  89 us
    all_to_all x2, starting transfers between devices, spectral(): lax.all_to_all(slab, 'gx', split_axis=1, concat_axis=0, tiled=True)  16.4 us
    dot_general x6, matrix products, per_device(): jnp.einsum('oc,xycz->xyoz', kernel_weight[tile], moved, preferred_element...  10.4 us
    all_to_all x2, starting transfers between devices, spectral(): return lax.all_to_all(result, 'gx', split_axis=0, concat_axis=1, tiled=True)  10.1 us
    dot_general x6, matrix products, per_device(): jnp.einsum('oc,xyoz->xycz', kernel_weight[tile], back_moved, preferred_el...  9.73 us
    all_to_all x2, waiting for transfers between devices, spectral(): return lax.all_to_all(result, 'gx', split_axis=0, concat_axis=1, tiled=True)  7.95 us
    dot_general x1, matrix products, per_device(): jnp.einsum('oc,xyoz->xycz', lap_weight, laplace_ext(ext_grad), preferred_...  7.47 us
    dot_general x6, matrix products, per_device(): jnp.einsum('xyoz,xycz->oc', back_moved, features, preferred_element_type=...  6.05 us
  transfers between devices with their start and end apart: 9, of which 3 were waited for; matrix products, arithmetic and copies ran while one was open for 14% of the time, Pallas kernels for 0%

commit v1 on v0

--- a/solution.py
+++ b/solution.py
@@ -92,6 +92,17 @@
     return pullback(upstream)[0]
 
 
+def sum_over_gx(terms):
+    count = lax.axis_size("gx")
+    if terms.size % count:
+        return lax.psum(terms, "gx")
+    pieces = lax.all_to_all(terms.reshape(count, -1), "gx", split_axis=0, concat_axis=0, tiled=True)
+    mine = jnp.sum(pieces, axis=0)
+    copies = jnp.broadcast_to(mine[None, :], pieces.shape)
+    gathered = lax.all_to_all(copies, "gx", split_axis=0, concat_axis=0, tiled=True)
+    return gathered.reshape(terms.shape)
+
+
 def per_device(
     features,
     cotangent,
@@ -150,7 +161,7 @@
     scaling = float(
         lax.axis_size("gx") * features.shape[0] * features.shape[1] * features.shape[3]
     ) ** (-0.5)
-    summed = lax.psum(local_grad, "gx")
+    summed = sum_over_gx(local_grad)
     return (input_grad.astype(jnp.bfloat16), summed * scaling)
 
 

time: 242 us -> 168 us (0.69)
  waiting for transfers between devices: 102 us -> 36.7 us
  between operations: 48.2 us -> 34.7 us
  starting transfers between devices: 33.4 us -> 40.5 us
  matrix products: 43.7 us -> 38.7 us
    psum x1 -> x0, waiting for transfers between devices: 89 us -> none  [per_device(): summed = lax.psum(local_grad, 'gx')]
    all_to_all x0 -> x2, waiting for transfers between devices: none -> 11.7 us  [the longest x1 6.57 us: sum_over_gx(): lax.all_to_all(terms.reshape(count, -1), 'gx', split_axis=0, concat_axis=...]
    all_to_all x0 -> x2, starting transfers between devices: none -> 10.9 us  [the longest x1 6.87 us: sum_over_gx(): lax.all_to_all(terms.reshape(count, -1), 'gx', split_axis=0, concat_axis=...]
    all_to_all x2, waiting for transfers between devices: 7.95 us -> 14.1 us  [spectral(): return lax.all_to_all(result, 'gx', split_axis=0, concat_axis=1, tiled=True)]
    all_to_all x2, waiting for transfers between devices: 4.71 us -> 10.8 us  [spectral(): lax.all_to_all(slab, 'gx', split_axis=1, concat_axis=0, tiled=True)]
    dot_general x6, matrix products: 6.05 us -> 2.37 us  [per_device(): jnp.einsum('xyoz,xycz->oc', back_moved, features, preferred_element_type=...]
    all_to_all x2, starting transfers between devices: 16.4 us -> 13.2 us  [spectral(): lax.all_to_all(slab, 'gx', split_axis=1, concat_axis=0, tiled=True)]
  transfers between devices with their start and end apart: 9 -> 10, of which waited for: 3 -> 5; matrix products, arithmetic and copies ran while one was open for 14% -> 18% of each run, Pallas kernels for 0% -> 0%
where the time goes in v1:
time: 168 us; the launch traced here: 166 us
  starting transfers between devices  40.5 us (24%)
  matrix products  38.7 us (23%)
  waiting for transfers between devices  36.7 us (22%)
  between operations  34.7 us (21%)
  local copies, waits for them, and re-layouts  10.6 us (6%)
  other arithmetic  5.23 us (3%)
    all_to_all x2, waiting for transfers between devices, spectral(): return lax.all_to_all(result, 'gx', split_axis=0, concat_axis=1, tiled=True)  14.1 us
    all_to_all x2, starting transfers between devices, spectral(): lax.all_to_all(slab, 'gx', split_axis=1, concat_axis=0, tiled=True)  13.2 us
    all_to_all x2, waiting for transfers between devices, spectral(): lax.all_to_all(slab, 'gx', split_axis=1, concat_axis=0, tiled=True)  10.8 us
    dot_general x6, matrix products, per_device(): jnp.einsum('oc,xycz->xyoz', kernel_weight[tile], moved, preferred_element...  10.4 us
    all_to_all x2, starting transfers between devices, spectral(): return lax.all_to_all(result, 'gx', split_axis=0, concat_axis=1, tiled=True)  9.56 us
    dot_general x6, matrix products, per_device(): jnp.einsum('oc,xyoz->xycz', kernel_weight[tile], back_moved, preferred_el...  9.38 us
    dot_general x1, matrix products, per_device(): jnp.einsum('oc,xyoz->xycz', lap_weight, laplace_ext(ext_grad), preferred_...  7.47 us
    all_to_all x1, starting transfers between devices, sum_over_gx(): lax.all_to_all(terms.reshape(count, -1), 'gx', split_axis=0, concat_axis=...  6.87 us
  transfers between devices with their start and end apart: 10, of which 5 were waited for; matrix products, arithmetic and copies ran while one was open for 18% of the time, Pallas kernels for 0%

profile of v1, /device:TPU:0, one launch (start us, length us, event | category | flops | bytes accessed | tf_op | source)
XLA Modules:
  0.0 166.4 jit_solution(13771764491910680602)
XLA Ops:
  0.7 1.1 fusion.148
  1.8 2.4 %collective-permute-start = (bf16[1,16,64,128]{3,2,1,0:T(8,128)(2,1)S(1)}, bf16[1,16,64,128]{3,2,1,0:T(8,128)(2,1)S(1)}, u32[]{:S(2)}, u32[]{:S(2)}) collective-permute-start(bf16[1,16,64,128]{3,2,1,0:T(8,128)(2,1)S(1)} %get-tuple-element.5), channel_id=1, source_target_pairs={{0,1},{1,2},{2,3},{3,4},{4,5},{5,6},{6,7},{7,8},{8,9},{9,10},{10,1... | collective-permute-start | bytes 786440 | tf_op jit(solution)/shard_map/ppermute | solution.py:20
  4.2 1.3 collective-permute-start.1
  5.5 1.9 %copy.40 = bf16[2,16,64,128]{3,2,0,1:T(8,128)(2,1)} copy(bf16[2,16,64,128]{3,2,1,0:T(8,128)(2,1)} %param.10) | data formatting | bytes 1048576 | tf_op args[0]
  7.4 9.4 %all-to-all-start = ((bf16[2,16,64,128]{3,2,0,1:T(8,128)(2,1)}), bf16[2,16,64,128]{3,2,0,1:T(8,128)(2,1)S(1)}, u32[]{:S(2)}, u32[]{:S(2)}) async-start(bf16[2,16,64,128]{3,2,0,1:T(8,128)(2,1)} %copy.40), calls=%async_computation | async-start | bytes 1048576 | tf_op jit(solution)/shard_map/all_to_all | solution.py:59
  16.9 1.3 fusion.76
  42.9 1.5 fusion.48
  44.4 1.4 fusion.49
  49.3 6.0 %all-to-all-start.1 = ((bf16[32,1,64,128]{3,2,1,0:T(8,128)(2,1)}), bf16[32,1,64,128]{3,2,1,0:T(8,128)(2,1)S(1)}, u32[]{:S(2)}, u32[]{:S(2)}) async-start(bf16[32,1,64,128]{3,2,1,0:T(8,128)(2,1)} %copy.44), calls=%async_computation.1 | async-start | bytes 1048576 | tf_op jit(solution)/shard_map/all_to_all | solution.py:64
  56.1 1.4 fusion.50
  57.5 1.4 fusion.51
  58.9 2.8 %convolution_add_fusion.1 = f32[2,16,128,64]{2,3,1,0:T(8,128)} fusion(f32[2,16,128,64]{2,3,1,0:T(8,128)S(1)} %copy-done.4, f32[4,18,64,130]{3,2,1,0:T(8,128)S(1)} %pad_convert_fusion.1, bf16[64,64]{1,0:T(8,128)(2,1)S(1)} %copy-done.15), kind=kOutput, calls=%fused_computation.37 | convolution fusion | flops 35913728 | bytes 9453568 | tf_op jit(solution)/shard_map/oc,xycz->xyoz/dot_general | solution.py:129
  61.8 8.0 %all-to-all-done.1 = bf16[32,1,64,128]{3,2,1,0:T(8,128)(2,1)S(1)} async-done(((bf16[32,1,64,128]{3,2,1,0:T(8,128)(2,1)}), bf16[32,1,64,128]{3,2,1,0:T(8,128)(2,1)S(1)}, u32[]{:S(2)}, u32[]{:S(2)}) %all-to-all-start.1) | async-done | bytes 524320 | tf_op jit(solution)/shard_map/all_to_all | solution.py:64
  70.5 4.2 %fusion.33 = bf16[2,16,64,128]{3,2,1,0:T(8,128)(2,1)S(1)} fusion(bf16[2,16,64,128]{3,2,1,0:T(8,128)(2,1)} %param.11, f32[2,16,128,64]{2,3,1,0:T(8,128)} %fusion.51, f32[2,16,128,64]{2,3,1,0:T(8,128)} %fusion.50, f32[2,16,128,64]{2,3,1,0:T(8,128)} %fusion.49, f32[2,16,128,64]{2,3,1,0:T(8,128)} %fusion.48, f32[2,16,128,64]{2,3,1,0:T(8,128)S(1)} %fusion.47, ...), kind=kOutput, calls=%fused_computation.72 | convolution fusion | flops 41680896 | bytes 8946188 | tf_op jit(solution)/shard_map/oc,xycz->xyoz/dot_general | solution.py:134
  74.8 1.9 %collective-permute-start.2 = (bf16[1,16,64,128]{3,2,1,0:T(8,128)(2,1)S(1)}, bf16[1,16,64,128]{3,2,1,0:T(8,128)(2,1)S(1)}, u32[]{:S(2)}, u32[]{:S(2)}) collective-permute-start(bf16[1,16,64,128]{3,2,1,0:T(8,128)(2,1)S(1)} %get-tuple-element.2), channel_id=1, source_target_pairs={{0,1},{1,2},{2,3},{3,4},{4,5},{5,6},{6,7},{7,8},{8,9},{9,10},{10,1... | collective-permute-start | bytes 786440 | tf_op jit(solution)/shard_map/ppermute | solution.py:20
  76.7 1.3 collective-permute-start.3
  92.6 6.9 %all-to-all-start.4 = ((f32[16,1,1536]{2,1,0:T(1,128)}), f32[16,1,1536]{2,1,0:T(1,128)S(1)}, u32[]{:S(2)}, u32[]{:S(2)}) async-start(f32[16,1,1536]{2,1,0:T(1,128)} %all_to_all.57), calls=%async_computation.4 | async-start | bytes 196608 | tf_op jit(solution)/shard_map/all_to_all | solution.py:99
  100.3 6.6 %all-to-all-done.4 = f32[16,1,1536]{2,1,0:T(1,128)S(1)} async-done(((f32[16,1,1536]{2,1,0:T(1,128)}), f32[16,1,1536]{2,1,0:T(1,128)S(1)}, u32[]{:S(2)}, u32[]{:S(2)}) %all-to-all-start.4) | async-done | bytes 98336 | tf_op jit(solution)/shard_map/all_to_all | solution.py:99
  107.6 3.8 %all-to-all-start.2 = ((bf16[2,16,64,128]{3,2,0,1:T(8,128)(2,1)}), bf16[2,16,64,128]{3,2,0,1:T(8,128)(2,1)S(1)}, u32[]{:S(2)}, u32[]{:S(2)}) async-start(bf16[2,16,64,128]{3,2,0,1:T(8,128)(2,1)} %copy.49), calls=%async_computation.2 | async-start | bytes 1048576 | tf_op jit(solution)/shard_map/all_to_all | solution.py:59
  111.4 1.3 fusion.74
  113.2 1.4 convolution_bitcast_fusion.2
  114.7 10.8 %all-to-all-done.2 = bf16[2,16,64,128]{3,2,0,1:T(8,128)(2,1)S(1)} async-done(((bf16[2,16,64,128]{3,2,0,1:T(8,128)(2,1)}), bf16[2,16,64,128]{3,2,0,1:T(8,128)(2,1)S(1)}, u32[]{:S(2)}, u32[]{:S(2)}) %all-to-all-start.2) | async-done | bytes 524320 | tf_op jit(solution)/shard_map/all_to_all | solution.py:59
  126.3 4.0 %all-to-all-start.5 = ((f32[16,1,1536]{2,1,0:T(1,128)}), f32[16,1,1536]{2,1,0:T(1,128)S(1)}, u32[]{:S(2)}, u32[]{:S(2)}) async-start(f32[16,1,1536]{2,1,0:T(1,128)} %broadcast_in_dim.14), calls=%async_computation.5 | async-start | bytes 196608 | tf_op jit(solution)/shard_map/all_to_all | solution.py:102
  132.5 5.2 %all-to-all-done.5 = f32[16,1,1536]{2,1,0:T(1,128)S(1)} async-done(((f32[16,1,1536]{2,1,0:T(1,128)}), f32[16,1,1536]{2,1,0:T(1,128)S(1)}, u32[]{:S(2)}, u32[]{:S(2)}) %all-to-all-start.5) | async-done | bytes 98336 | tf_op jit(solution)/shard_map/all_to_all | solution.py:102
  137.7 3.6 %all-to-all-start.3 = ((bf16[32,1,64,128]{3,2,1,0:T(8,128)(2,1)}), bf16[32,1,64,128]{3,2,1,0:T(8,128)(2,1)S(1)}, u32[]{:S(2)}, u32[]{:S(2)}) async-start(bf16[32,1,64,128]{3,2,1,0:T(8,128)(2,1)} %copy.55), calls=%async_computation.3 | async-start | bytes 1048576 | tf_op jit(solution)/shard_map/all_to_all | solution.py:64
  141.3 2.9 %pad_convert_fusion = f32[4,18,64,130]{3,2,1,0:T(8,128)} fusion(bf16[4,16,64,128]{3,2,1,0:T(8,128)(2,1)S(1)} %pad_maximum_fusion), kind=kLoop, calls=%fused_computation.12 | loop fusion | flops 599040 | bytes 3444736 | tf_op jit(solution)/shard_map/convert_element_type | solution.py:68
  144.2 1.4 convolution_bitcast_fusion.3
  145.6 1.5 convolution_bitcast_fusion.4
  147.1 1.4 convolution_bitcast_fusion
  149.5 6.2 %all-to-all-done.3 = bf16[32,1,64,128]{3,2,1,0:T(8,128)(2,1)S(1)} async-done(((bf16[32,1,64,128]{3,2,1,0:T(8,128)(2,1)}), bf16[32,1,64,128]{3,2,1,0:T(8,128)(2,1)S(1)}, u32[]{:S(2)}, u32[]{:S(2)}) %all-to-all-start.3) | async-done | bytes 524320 | tf_op jit(solution)/shard_map/all_to_all | solution.py:64
  155.7 7.5 %fusion.15 = f32[2,16,64,128]{3,2,1,0:T(8,128)S(1)} fusion(f32[2,16,128,64]{2,3,1,0:T(8,128)} %fusion.74, f32[4,18,64,130]{3,2,1,0:T(8,128)} %pad_convert_fusion, bf16[64,64]{1,0:T(8,128)(2,1)S(1)} %copy-done.16, bf16[16,2,1,64,128]{4,3,1,0,2:T(8,128)(2,1)S(1)} %bitcast.307), kind=kOutput, calls=%fused_computation.40 | convolution fusion | flops 36438016 | bytes 9969664 | tf_op jit(solution)/shard_map/oc,xyoz->xycz/dot_general | solution.py:147
  163.2 3.2 %fusion.16 = bf16[2,16,64,128]{3,2,1,0:T(8,128)(2,1)} fusion(f32[2,16,64,128]{3,2,1,0:T(8,128)S(1)} %copy-done.2, f32[2,16,64,128]{3,2,1,0:T(8,128)S(1)} %convolution_bitcast_fusion.1, f32[2,16,64,128]{3,2,1,0:T(8,128)} %convolution_bitcast_fusion.2, f32[2,16,64,128]{3,2,1,0:T(8,128)} %convolution_bitcast_fusion.3, ...), kind=kOutput, calls=%fused_computation.43 | convolution fusion | flops 35389440 | bytes 7880716 | tf_op jit(solution)/shard_map/oc,xyoz->xycz/dot_general | solution.py:154
  (73 shorter events, 16.8 us)
Async XLA Ops:
  0.6 46.3 %copy-start = (bf16[16,64,64]{2,1,0:T(8,128)(2,1)S(1)}, bf16[16,64,64]{2,1,0:T(8,128)(2,1)}, u32[]{:S(2)}) copy-start(bf16[16,64,64]{2,1,0:T(8,128)(2,1)} %param.18) | copy-start | bytes 393220
  0.6 16.2 %copy-start.1 = (bf16[2,16,64,128]{3,2,1,0:T(8,128)(2,1)S(1)}, bf16[2,16,64,128]{3,2,1,0:T(8,128)(2,1)}, u32[]{:S(2)}) copy-start(bf16[2,16,64,128]{3,2,1,0:T(8,128)(2,1)} %param.10) | copy-start | bytes 1572868
  0.7 16.2 %copy-start.14 = (s32[64]{0:T(128)S(1)}, s32[64]{0:T(128)}, u32[]{:S(2)}) copy-start(s32[64]{0:T(128)} %param.13) | copy-start | bytes 772
  0.7 16.2 %copy-start.8 = (bf16[64,64]{1,0:T(8,128)(2,1)S(1)}, bf16[64,64]{1,0:T(8,128)(2,1)}, u32[]{:S(2)}) copy-start(bf16[64,64]{1,0:T(8,128)(2,1)} %param.15) | copy-start | bytes 24580
  0.7 17.4 %copy-start.10 = (s32[2,16,128]{2,1,0:T(8,128)S(1)}, s32[2,16,128]{2,1,0:T(8,128)}, u32[]{:S(2)}) copy-start(s32[2,16,128]{2,1,0:T(8,128)} %param.12) | copy-start | bytes 49156
  0.7 18.0 %copy-start.9 = (s32[6,3]{0,1:T(4,128)S(1)}, s32[6,3]{0,1:T(4,128)}, u32[]{:S(2)}) copy-start(s32[6,3]{0,1:T(4,128)} %param.14) | copy-start | bytes 220
  1.8 40.5 %collective-permute-start = (bf16[1,16,64,128]{3,2,1,0:T(8,128)(2,1)S(1)}, bf16[1,16,64,128]{3,2,1,0:T(8,128)(2,1)S(1)}, u32[]{:S(2)}, u32[]{:S(2)}) collective-permute-start(bf16[1,16,64,128]{3,2,1,0:T(8,128)(2,1)S(1)} %get-tuple-element.5), channel_id=1, source_target_pairs={{0,1},{1,2},{2,3},{3,4},{4,5},{5,6},{6,7},{7,8},{8,9},{9,10},{10,1... | collective-permute-start | bytes 786440 | tf_op jit(solution)/shard_map/ppermute | solution.py:20
  4.2 38.2 %collective-permute-start.1 = (bf16[1,16,64,128]{3,2,1,0:T(8,128)(2,1)S(1)}, bf16[1,16,64,128]{3,2,1,0:T(8,128)(2,1)S(1)}, u32[]{:S(2)}, u32[]{:S(2)}) collective-permute-start(bf16[1,16,64,128]{3,2,1,0:T(8,128)(2,1)S(1)} %get-tuple-element.4), channel_id=1, source_target_pairs={{1,0},{2,1},{3,2},{4,3},{5,4},{6,5},{7,6},{8,7},{9,8},{10,9},{11,1... | collective-permute-start | bytes 786440 | tf_op jit(solution)/shard_map/ppermute | solution.py:22
  7.4 35.1 %copy-start.5 = (bf16[6,64,64]{2,1,0:T(8,128)(2,1)S(1)}, bf16[6,64,64]{2,1,0:T(8,128)(2,1)}, u32[]{:S(2)}) copy-start(bf16[6,64,64]{2,1,0:T(8,128)(2,1)} %param.16) | copy-start | bytes 147460
  7.4 38.4 %all-to-all-start = ((bf16[2,16,64,128]{3,2,0,1:T(8,128)(2,1)}), bf16[2,16,64,128]{3,2,0,1:T(8,128)(2,1)S(1)}, u32[]{:S(2)}, u32[]{:S(2)}) async-start(bf16[2,16,64,128]{3,2,0,1:T(8,128)(2,1)} %copy.40), calls=%async_computation | async-start | bytes 1048576 | tf_op jit(solution)/shard_map/all_to_all | solution.py:59
  49.3 20.5 %all-to-all-start.1 = ((bf16[32,1,64,128]{3,2,1,0:T(8,128)(2,1)}), bf16[32,1,64,128]{3,2,1,0:T(8,128)(2,1)S(1)}, u32[]{:S(2)}, u32[]{:S(2)}) async-start(bf16[32,1,64,128]{3,2,1,0:T(8,128)(2,1)} %copy.44), calls=%async_computation.1 | async-start | bytes 1048576 | tf_op jit(solution)/shard_map/all_to_all | solution.py:64
  56.0 2.9 %copy-start.4 = (f32[2,16,128,64]{2,3,1,0:T(8,128)S(1)}, f32[2,16,128,64]{2,3,1,0:T(8,128)}, u32[]{:S(2)}) copy-start(f32[2,16,128,64]{2,3,1,0:T(8,128)} %fusion.76) | copy-start | bytes 3145732
  56.1 2.9 %copy-start.15 = (bf16[64,64]{1,0:T(8,128)(2,1)S(1)}, bf16[64,64]{1,0:T(8,128)(2,1)}, u32[]{:S(2)}) copy-start(bf16[64,64]{1,0:T(8,128)(2,1)} %param.17) | copy-start | bytes 24580
  57.5 13.0 %copy-start.13 = (f32[64]{0:T(128)S(1)}, f32[64]{0:T(128)}, u32[]{:S(2)}) copy-start(f32[64]{0:T(128)} %param.19) | copy-start | bytes 772
  69.7 0.8 copy-start.3
  74.8 14.5 %collective-permute-start.2 = (bf16[1,16,64,128]{3,2,1,0:T(8,128)(2,1)S(1)}, bf16[1,16,64,128]{3,2,1,0:T(8,128)(2,1)S(1)}, u32[]{:S(2)}, u32[]{:S(2)}) collective-permute-start(bf16[1,16,64,128]{3,2,1,0:T(8,128)(2,1)S(1)} %get-tuple-element.2), channel_id=1, source_target_pairs={{0,1},{1,2},{2,3},{3,4},{4,5},{5,6},{6,7},{7,8},{8,9},{9,10},{10,1... | collective-permute-start | bytes 786440 | tf_op jit(solution)/shard_map/ppermute | solution.py:20
  76.7 12.6 %collective-permute-start.3 = (bf16[1,16,64,128]{3,2,1,0:T(8,128)(2,1)S(1)}, bf16[1,16,64,128]{3,2,1,0:T(8,128)(2,1)S(1)}, u32[]{:S(2)}, u32[]{:S(2)}) collective-permute-start(bf16[1,16,64,128]{3,2,1,0:T(8,128)(2,1)S(1)} %get-tuple-element.3), channel_id=1, source_target_pairs={{1,0},{2,1},{3,2},{4,3},{5,4},{6,5},{7,6},{8,7},{9,8},{10,9},{11,1... | collective-permute-start | bytes 786440 | tf_op jit(solution)/shard_map/ppermute | solution.py:22
  92.6 14.3 %all-to-all-start.4 = ((f32[16,1,1536]{2,1,0:T(1,128)}), f32[16,1,1536]{2,1,0:T(1,128)S(1)}, u32[]{:S(2)}, u32[]{:S(2)}) async-start(f32[16,1,1536]{2,1,0:T(1,128)} %all_to_all.57), calls=%async_computation.4 | async-start | bytes 196608 | tf_op jit(solution)/shard_map/all_to_all | solution.py:99
  106.9 0.6 copy-start.6
  107.6 18.0 %all-to-all-start.2 = ((bf16[2,16,64,128]{3,2,0,1:T(8,128)(2,1)}), bf16[2,16,64,128]{3,2,0,1:T(8,128)(2,1)S(1)}, u32[]{:S(2)}, u32[]{:S(2)}) async-start(bf16[2,16,64,128]{3,2,0,1:T(8,128)(2,1)} %copy.49), calls=%async_computation.2 | async-start | bytes 1048576 | tf_op jit(solution)/shard_map/all_to_all | solution.py:59
  112.8 1.9 %copy-start.7 = (f32[16,1,1536]{2,1,0:T(1,128)S(1)}, f32[16,1,1536]{2,1,0:T(1,128)}, u32[]{:S(2)}) copy-start(f32[16,1,1536]{2,1,0:T(1,128)} %copy-done.6) | copy-start | bytes 294916
  112.8 17.5 %copy-start.11 = (f32[16]{0:T(128)S(1)}, f32[16]{0:T(128)}, u32[]{:S(2)}) copy-start(f32[16]{0:T(128)} %get-tuple-element.27) | copy-start | bytes 196
  112.8 17.5 %copy-start.12 = (f32[32]{0:T(128)S(1)}, f32[32]{0:T(128)}, u32[]{:S(2)}) copy-start(f32[32]{0:T(128)} %multiply_add_fusion) | copy-start | bytes 388
  126.3 11.4 %all-to-all-start.5 = ((f32[16,1,1536]{2,1,0:T(1,128)}), f32[16,1,1536]{2,1,0:T(1,128)S(1)}, u32[]{:S(2)}, u32[]{:S(2)}) async-start(f32[16,1,1536]{2,1,0:T(1,128)} %broadcast_in_dim.14), calls=%async_computation.5 | async-start | bytes 196608 | tf_op jit(solution)/shard_map/all_to_all | solution.py:102
  137.7 18.0 %all-to-all-start.3 = ((bf16[32,1,64,128]{3,2,1,0:T(8,128)(2,1)}), bf16[32,1,64,128]{3,2,1,0:T(8,128)(2,1)S(1)}, u32[]{:S(2)}, u32[]{:S(2)}) async-start(bf16[32,1,64,128]{3,2,1,0:T(8,128)(2,1)} %copy.55), calls=%async_computation.3 | async-start | bytes 1048576 | tf_op jit(solution)/shard_map/all_to_all | solution.py:64
  145.6 10.1 %copy-start.16 = (bf16[64,64]{1,0:T(8,128)(2,1)S(1)}, bf16[64,64]{1,0:T(8,128)(2,1)}, u32[]{:S(2)}) copy-start(bf16[64,64]{1,0:T(8,128)(2,1)} %param.17) | copy-start | bytes 24580
  155.7 7.5 %copy-start.2 = (f32[2,16,64,128]{3,2,1,0:T(8,128)S(1)}, f32[2,16,64,128]{3,2,1,0:T(8,128)}, u32[]{:S(2)}) copy-start(f32[2,16,64,128]{3,2,1,0:T(8,128)} %convolution_bitcast_fusion) | copy-start | bytes 3145732

commit v2 on v1

--- a/solution.py
+++ b/solution.py
@@ -1,12 +1,16 @@
+import functools
 from functools import partial
 import math
 
 import jax
 import jax.numpy as jnp
 from jax import lax
+from jax.experimental import pallas as pl
+from jax.experimental.pallas import tpu as pltpu
 from jax.sharding import PartitionSpec as P
 
 RAD = 2
+MESH = pl.DeviceIdType.MESH
 
 
 def with_halo(cells, sides, width):
@@ -165,9 +169,417 @@
     return (input_grad.astype(jnp.bfloat16), summed * scaling)
 
 
+def fused_kernel(
+    count,
+    feat,
+    cot,
+    wall,
+    offs,
+    basis,
+    wf,
+    wb,
+    wm,
+    wmt,
+    bias,
+    out,
+    kout,
+    zs,
+    cat,
+    local,
+    acc,
+    vh,
+    pen1,
+    pen2,
+    stage1,
+    stage2,
+    spec1,
+    spec2,
+    wgt,
+    halo1,
+    halo2,
+    kacc,
+    kpart,
+    ksum,
+    kall,
+    send,
+    recv,
+    hsend,
+    hrecv,
+):
+    me = lax.axis_index("gx")
+    grp = lax.axis_index("groups")
+    xl, ny, ch, nz = feat.shape
+    modes = wm.shape[0]
+    tiles = offs.shape[0]
+    f32, bf16 = jnp.float32, jnp.bfloat16
+
+    def remote(src, dst, phase, d, peer):
+        return pltpu.make_async_remote_copy(
+            src_ref=src,
+            dst_ref=dst,
+            send_sem=send.at[phase, d],
+            recv_sem=recv.at[phase, d],
+            device_id=(grp, peer),
+            device_id_type=MESH,
+        )
+
+    def ahead(d):
+        return lax.rem(me + d, count)
+
+    def behind(d):
+        return lax.rem(me + count - d, count)
+
+    def halo_copy(src, dst, slot, peer):
+        return pltpu.make_async_remote_copy(
+            src_ref=src,
+            dst_ref=dst,
+            send_sem=hsend.at[slot],
+            recv_sem=hrecv.at[slot],
+            device_id=(grp, peer),
+            device_id_type=MESH,
+        )
+
+    def each(low, high, body):
+        def step(i, carry):
+            body(i)
+            return carry
+
+        lax.fori_loop(low, high, step, 0)
+
+    barrier = pltpu.get_barrier_semaphore()
+    each(
+        1,
+        count,
+        lambda d: pl.semaphore_signal(
+            barrier, inc=1, device_id=(grp, ahead(d)), device_id_type=MESH
+        ),
+    )
+    pl.semaphore_wait(barrier, count - 1)
+
+    def halo_start(low_plane, high_plane, halo, base):
+        @pl.when(me > 0)
+        def _():
+            halo_copy(low_plane, halo.at[1], base, me - 1).start()
+
+        @pl.when(me < count - 1)
+        def _():
+            halo_copy(high_plane, halo.at[0], base + 1, me + 1).start()
+
+        @pl.when(me == 0)
+        def _():
+            halo[0] = jnp.zeros(halo.shape[1:], bf16)
+
+        @pl.when(me == count - 1)
+        def _():
+            halo[1] = jnp.zeros(halo.shape[1:], bf16)
+
+    def halo_wait(low_plane, high_plane, halo, base):
+        @pl.when(me > 0)
+        def _():
+            halo_copy(low_plane, halo.at[1], base, me - 1).wait_send()
+            halo_copy(high_plane, halo.at[0], base + 1, me - 1).wait_recv()
+
+        @pl.when(me < count - 1)
+        def _():
+            halo_copy(high_plane, halo.at[0], base + 1, me + 1).wait_send()
+            halo_copy(low_plane, halo.at[1], base, me + 1).wait_recv()
+
+    lane = lax.broadcasted_iota(jnp.int32, (ch, nz), 1)
+
+    def spread(load, place):
+        def body(y):
+            v = load(y)
+            zs[RAD, place, y + RAD] = v
+            wide = v.astype(f32)
+            for dz in range(-RAD, RAD + 1):
+                if dz:
+                    moved = pltpu.roll(wide, (-dz) % nz, 1)
+                    inside = lane < nz - dz if dz > 0 else lane >= -dz
+                    zs[RAD + dz, place, y + RAD] = jnp.where(inside, moved, 0.0).astype(bf16)
+
+        each(0, ny, body)
+
+    def gather_rows(direction):
+        def body(y):
+            for x in range(xl):
+                lanes = slice(x * nz, (x + 1) * nz)
+                centre = zs[RAD, x + 1, y + RAD]
+                cat[y, 0:ch, lanes] = centre
+                total = zs[RAD, x + 2, y + RAD].astype(f32) + zs[RAD, x, y + RAD].astype(f32)
+                total = total + zs[RAD, x + 1, y + RAD + 1].astype(f32)
+                total = total + zs[RAD, x + 1, y + RAD - 1].astype(f32)
+                total = total + zs[RAD + 1, x + 1, y + RAD].astype(f32)
+                total = total + zs[RAD - 1, x + 1, y + RAD].astype(f32)
+                cat[y, ch : 2 * ch, lanes] = (total - 6.0 * centre.astype(f32)).astype(bf16)
+                for t in range(tiles):
+                    moved = zs[
+                        RAD + direction * offs[t, 2],
+                        x + 1 + direction * offs[t, 0],
+                        y + RAD + direction * offs[t, 1],
+                    ]
+                    cat[y, (2 + t) * ch : (3 + t) * ch, lanes] = moved
+
+        each(0, ny, body)
+
+    def mix(weights):
+        def body(y):
+            local[y] = jnp.dot(weights[...], cat[y], preferred_element_type=f32)
+
+        each(0, ny, body)
+
+    def gain(planes, src):
+        wide = [p.astype(f32) for p in planes]
+        for k in range(modes):
+            total = acc[k]
+            for j in range(xl):
+                total = total + basis[k, src * xl + j] * wide[j]
+            acc[k] = total
+
+    def channel_mix(weights):
+        for k in range(modes):
+            u = acc[k].astype(bf16)
+            v = jnp.dot(weights[k], u, preferred_element_type=f32)
+            vh[k] = v.astype(bf16).astype(f32)
+
+    def expand(stage, peer):
+        for j in range(xl):
+            total = basis[0, peer * xl + j] * vh[0]
+            for k in range(1, modes):
+                total = total + basis[k, peer * xl + j] * vh[k]
+            stage[peer, j] = total.astype(bf16)
+
+    each(1, count, lambda d: remote(feat.at[:, ahead(d)], pen1.at[me], 0, d, ahead(d)).start())
+    low1, high1 = feat.at[0], feat.at[xl - 1]
+    halo_start(low1, high1, halo1, 0)
+
+    for edge in (0, RAD + ny):
+        for dz in range(2 * RAD + 1):
+            for x in range(xl + 2):
+                zs[dz, x, edge : edge + RAD] = jnp.zeros((RAD, ch, nz), bf16)
+    for x in range(xl):
+        spread(lambda y: feat[x, y], x + 1)
+    acc[...] = jnp.zeros(acc.shape, f32)
+    gain([feat[j, me] for j in range(xl)], me)
+    halo_wait(low1, high1, halo1, 0)
+    spread(lambda y: halo1[0, y], 0)
+    spread(lambda y: halo1[1, y], xl + 1)
+    gather_rows(1)
+
+    def take1(d):
+        src = behind(d)
+        remote(feat.at[:, src], pen1.at[src], 0, d, src).wait_recv()
+        gain([pen1[src, j] for j in range(xl)], src)
+
+    each(1, count, take1)
+    channel_mix(wm)
+
+    def give1(d):
+        peer = ahead(d)
+        expand(stage1, peer)
+        remote(stage1.at[peer], spec1.at[me], 1, d, peer).start()
+
+    each(1, count, give1)
+    expand(stage1, me)
+    mix(wf)
+    root = math.sqrt(2.0 / math.pi)
+
+    def slope(y, planes):
+        for x in range(xl):
+            v = local[y, :, x * nz : (x + 1) * nz] + planes[x].astype(f32) + bias[...]
+            square = v * v
+            t = jnp.tanh(root * (v + 0.044715 * (square * v)))
+            g = 0.5 * (1.0 + t)
+            g = g + (0.5 * v) * ((1.0 - t * t) * (root * (1.0 + (3.0 * 0.044715) * square)))
+            fluid = (1 - wall[x, pl.ds(y, 1), :]).astype(f32)
+            wgt[y, x] = ((cot[x, y].astype(f32) * g) * fluid).astype(bf16)
+
+    slope(me, [stage1[me, j] for j in range(xl)])
+
+    def turn(d):
+        src = behind(d)
+        remote(stage1.at[src], spec1.at[src], 1, d, src).wait_recv()
+        slope(src, [spec1[src, j] for j in range(xl)])
+        remote(wgt.at[src], pen2.at[me], 2, count - d, src).start()
+
+    each(1, count, turn)
+
+    low2, high2 = wgt.at[:, 0], wgt.at[:, xl - 1]
+    halo_start(low2, high2, halo2, 2)
+    for x in range(xl):
+        spread(lambda y: wgt[y, x], x + 1)
+    acc[...] = jnp.zeros(acc.shape, f32)
+    gain([wgt[me, j] for j in range(xl)], me)
+    halo_wait(low2, high2, halo2, 2)
+    spread(lambda y: halo2[0, y], 0)
+    spread(lambda y: halo2[1, y], xl + 1)
+    gather_rows(-1)
+
+    def take2(i):
+        d = count - i
+        src = behind(d)
+        remote(wgt.at[src], pen2.at[src], 2, d, src).wait_recv()
+        gain([pen2[src, j] for j in range(xl)], src)
+
+    each(1, count, take2)
+    channel_mix(wmt)
+
+    def give2(d):
+        peer = ahead(d)
+        expand(stage2, peer)
+        remote(stage2.at[peer], spec2.at[me], 3, d, peer).start()
+
+    each(1, count, give2)
+    expand(stage2, me)
+
+    kacc[...] = jnp.zeros(kacc.shape, f32)
+
+    def tile_grad(y):
+        field = jnp.concatenate([feat[x, y] for x in range(xl)], axis=1)
+        kacc[...] += lax.dot_general(
+            cat[y, 2 * ch :, :], field, (((1,), (1,)), ((), ())), preferred_element_type=f32
+        )
+
+    each(0, ny, tile_grad)
+    rows = kpart.shape[1]
+    for p in range(count):
+        kpart[p] = kacc[p * rows : (p + 1) * rows]
+    each(1, count, lambda d: remote(kpart.at[ahead(d)], ksum.at[me], 4, d, ahead(d)).start())
+    mix(wb)
+    ksum[me] = kpart[me]
+    each(1, count, lambda d: remote(kpart.at[0], ksum.at[behind(d)], 4, d, behind(d)).wait_recv())
+    total = ksum[0]
+    for p in range(1, count):
+        total = total + ksum[p]
+    kall[me] = total * (float(count * xl * ny * nz) ** -0.5)
+    each(1, count, lambda d: remote(kall.at[me], kall.at[me], 5, d, ahead(d)).start())
+
+    def finish(y, planes):
+        for x in range(xl):
+            total = local[y, :, x * nz : (x + 1) * nz] + planes[x].astype(f32)
+            out[x, y] = total.astype(bf16)
+
+    finish(me, [stage2[me, j] for j in range(xl)])
+
+    def last(d):
+        src = behind(d)
+        remote(stage2.at[src], spec2.at[src], 3, d, src).wait_recv()
+        finish(src, [spec2[src, j] for j in range(xl)])
+
+    each(1, count, last)
+    each(1, count, lambda d: remote(kall.at[me], kall.at[behind(d)], 5, d, behind(d)).wait_recv())
+    kout[...] = kall[...]
+
+    def drain(d):
+        peer = ahead(d)
+        remote(feat.at[:, peer], pen1.at[me], 0, d, peer).wait_send()
+        remote(stage1.at[peer], spec1.at[me], 1, d, peer).wait_send()
+        remote(wgt.at[peer], pen2.at[me], 2, d, peer).wait_send()
+        remote(stage2.at[peer], spec2.at[me], 3, d, peer).wait_send()
+        remote(kpart.at[peer], ksum.at[me], 4, d, peer).wait_send()
+        remote(kall.at[me], kall.at[me], 5, d, peer).wait_send()
+
+    each(1, count, drain)
+
+
+def fits_kernel(count, features, kernel_weight):
+    xl, ny, ch, nz = features.shape
+    cells = xl * ny * ch * nz
+    tile_rows = kernel_weight.shape[0] * ch
+    if ny != count or nz % 128 or ch % 16 or tile_rows % (8 * count):
+        return False
+    return 80 * cells < 24 * 2**20
+
+
+def fused_device(
+    features,
+    cotangent,
+    wall_flags,
+    mode_counts,
+    offsets,
+    point_weight,
+    kernel_weight,
+    lap_weight,
+    spec_weight,
+    bias,
+):
+    count = lax.axis_size("gx")
+    if not fits_kernel(count, features, kernel_weight):
+        return per_device(
+            features,
+            cotangent,
+            wall_flags,
+            mode_counts,
+            offsets,
+            point_weight,
+            kernel_weight,
+            lap_weight,
+            spec_weight,
+            bias,
+        )
+    xl, ny, ch, nz = features.shape
+    modes, tiles = spec_weight.shape[0], kernel_weight.shape[0]
+    kept = jnp.arange(modes, dtype=jnp.int32)[:, None] < mode_counts[None, :]
+    masked = jnp.where(kept[:, :, None], spec_weight, jnp.zeros_like(spec_weight))
+    stacked = jnp.concatenate([point_weight[None], lap_weight[None], kernel_weight], axis=0)
+    forward = jnp.transpose(stacked, (1, 0, 2)).reshape(ch, (2 + tiles) * ch)
+    backward = jnp.transpose(stacked, (2, 0, 1)).reshape(ch, (2 + tiles) * ch)
+    rows = tiles * ch // count
+    f32, bf16 = jnp.float32, jnp.bfloat16
+    vmem = pl.BlockSpec(memory_space=pltpu.VMEM)
+    smem = pl.BlockSpec(memory_space=pltpu.SMEM)
+    field_grad, tile_grad = pl.pallas_call(
+        functools.partial(fused_kernel, count),
+        out_shape=(
+            jax.ShapeDtypeStruct(features.shape, bf16),
+            jax.ShapeDtypeStruct((count, rows, ch), f32),
+        ),
+        in_specs=[vmem, vmem, vmem, smem, smem, vmem, vmem, vmem, vmem, vmem],
+        out_specs=(vmem, vmem),
+        scratch_shapes=[
+            pltpu.VMEM((2 * RAD + 1, xl + 2, ny + 2 * RAD, ch, nz), bf16),
+            pltpu.VMEM((ny, (2 + tiles) * ch, xl * nz), bf16),
+            pltpu.VMEM((ny, ch, xl * nz), f32),
+            pltpu.VMEM((modes, ch, nz), f32),
+            pltpu.VMEM((modes, ch, nz), f32),
+            pltpu.VMEM((count, xl, ch, nz), bf16),
+            pltpu.VMEM((count, xl, ch, nz), bf16),
+            pltpu.VMEM((count, xl, ch, nz), bf16),
+            pltpu.VMEM((count, xl, ch, nz), bf16),
+            pltpu.VMEM((count, xl, ch, nz), bf16),
+            pltpu.VMEM((count, xl, ch, nz), bf16),
+            pltpu.VMEM((ny, xl, ch, nz), bf16),
+            pltpu.VMEM((2, ny, ch, nz), bf16),
+            pltpu.VMEM((2, ny, ch, nz), bf16),
+            pltpu.VMEM((tiles * ch, ch), f32),
+            pltpu.VMEM((count, rows, ch), f32),
+            pltpu.VMEM((count, rows, ch), f32),
+            pltpu.VMEM((count, rows, ch), f32),
+            pltpu.SemaphoreType.DMA((6, count)),
+            pltpu.SemaphoreType.DMA((6, count)),
+            pltpu.SemaphoreType.DMA((4,)),
+            pltpu.SemaphoreType.DMA((4,)),
+        ],
+        compiler_params=pltpu.CompilerParams(
+            collective_id=0, has_side_effects=True, vmem_limit_bytes=48 * 2**20
+        ),
+    )(
+        features,
+        cotangent,
+        wall_flags,
+        offsets,
+        basis_table(modes, count * xl).astype(f32),
+        forward,
+        backward,
+        masked,
+        jnp.swapaxes(masked, 1, 2),
+        jnp.broadcast_to(bias[:, None], (ch, nz)),
+    )
+    return field_grad, tile_grad.reshape(kernel_weight.shape)
+
+
 def solution(mesh):
     return jax.shard_map(
-        per_device,
+        fused_device,
         mesh=mesh,
         in_specs=(
             P(("groups", "gx"), None, None, None),

time: 168 us -> 90 us (0.54)
  Pallas kernels: 0 us -> 82.2 us
  starting transfers between devices: 40.5 us -> 0 us
  matrix products: 38.7 us -> 0 us
  waiting for transfers between devices: 36.7 us -> 0 us
  between operations: 34.7 us -> 0.77 us
  other arithmetic: 5.23 us -> 0.23 us
  local copies, waits for them, and re-layouts: 10.6 us -> 5.95 us
    pallas_call x0 -> x1, Pallas kernels: none -> 82.2 us  [fused_device(): pl.pallas_call(functools.partial(fused_kernel, count), out_shape=(jax.Sha...]
    dot_general x28 -> x0, matrix products: 38.7 us -> none  [the longest x6 10.4 us: per_device(): jnp.einsum('oc,xycz->xyoz', kernel_weight[tile], moved, preferred_element...]
    all_to_all x6 -> x0, waiting for transfers between devices: 36.7 us -> none  [the longest x2 14.1 us: spectral(): return lax.all_to_all(result, 'gx', split_axis=0, concat_axis=1, tiled=True)]
    all_to_all x6 -> x0, starting transfers between devices: 33.6 us -> none  [the longest x2 13.2 us: spectral(): lax.all_to_all(slab, 'gx', split_axis=1, concat_axis=0, tiled=True)]
    ppermute x4 -> x0, starting transfers between devices: 6.89 us -> none  [the longest x2 4.31 us: with_halo(): lax.ppermute(tail, axis, [(i, (i + 1) % count) for i in range(ends)])]
    convert_element_type x4 -> x1, other arithmetic: 3.7 us -> 0.12 us  [fused_device(): basis_table(modes, count * xl).astype(f32)]
    convert_element_type x4 -> x0, local copies, waits for them, and re-layouts: 2.94 us -> none  [the longest x2 2 us: pencil_work(): return jnp.einsum('kx,kyoz->xyoz', basis, mixed_modes, preferred_element_...]
    unnamed x37 -> x22, local copies, waits for them, and re-layouts: 3.47 us -> 5.38 us
  transfers between devices with their start and end apart: 10 -> 0, of which waited for: 5 -> 0; matrix products, arithmetic and copies ran while one was open for 18% -> 0% of each run, Pallas kernels for 0% -> 0%
where the time goes in v2:
time: 90 us; the launch traced here: 89.1 us
  Pallas kernels  82.2 us (91%)
  local copies, waits for them, and re-layouts  5.95 us (7%)
    pallas_call x1, Pallas kernels, fused_device(): pl.pallas_call(functools.partial(fused_kernel, count), out_shape=(jax.Sha...  82.2 us
    unnamed x22, local copies, waits for them, and re-layouts  5.38 us

profile of v2, /device:TPU:0, one launch (start us, length us, event | category | flops | bytes accessed | tf_op | source)
XLA Modules:
  0.0 89.1 jit_solution(13236825082529210596)
XLA Ops:
  0.7 0.0 copy-start.8
  0.7 0.0 copy-start.6
  0.7 0.6 copy-done.8
  1.3 0.0 copy-done.6
  1.4 0.1 copy.15.offs
  1.4 0.0 copy-start.7
  1.5 0.1 fusion.basis
  1.6 0.5 copy-done.7
  2.1 0.1 broadcast_in_dim.42.bias
  2.2 1.1 %copy.14 = bf16[16,64,64]{1,2,0:T(8,128)(2,1)S(1)} copy(bf16[16,64,64]{2,1,0:T(8,128)(2,1)} %param.18) | data formatting | bytes 262144 | tf_op args[8]
  3.4 0.0 copy-start.3
  3.4 0.0 copy-start.4
  3.4 0.0 copy-start.5
  3.4 0.0 copy-start.2
  3.4 0.2 copy.16.wm
  3.6 0.7 copy-done.3
  4.3 0.0 copy-done.4
  4.3 0.0 copy-done.5
  4.3 0.0 copy-start
  4.3 0.0 copy-start.1
  4.3 0.1 copy.17.wb
  4.4 0.1 copy.12
  4.5 0.1 reshape.51.wf
  4.7 0.0 copy-done.2
  4.7 0.6 copy-done
  5.3 0.2 copy-done.1
  5.5 82.2 %shard_map.113 = (bf16[2,16,64,128]{3,2,1,0:T(8,128)(2,1)S(1)}, f32[16,24,64]{2,1,0:T(8,128)S(1)}) custom-call(bf16[2,16,64,128]{3,2,1,0:T(8,128)(2,1)S(1)} %copy-done, bf16[2,16,64,128]{3,2,1,0:T(8,128)(2,1)S(1)} %copy-done.1, s32[2,16,128]{2,1,0:T(8,128)S(1)} %copy-done.2, s32[6,3]{1,0:T(8,128)S(1)} %copy.15.offs, f32[16,32]{1,0:T(8,128)S(1)} %fusion.basis, ...), custom_call_target="tpu_custom_call" | custom-call | tf_op jit(solution)/shard_map/pallas_call | solution.py:530
  87.7 0.8 copy.20
  88.5 0.7 copy.21
  (6 shorter events, 0.1 us)
Async XLA Ops:
  0.7 0.7 copy-start.8
  0.7 0.7 copy-start.6
  1.4 0.7 copy-start.7
  3.4 0.9 %copy-start.3 = (bf16[6,64,64]{2,1,0:T(8,128)(2,1)S(1)}, bf16[6,64,64]{2,1,0:T(8,128)(2,1)}, u32[]{:S(2)}) copy-start(bf16[6,64,64]{2,1,0:T(8,128)(2,1)} %param.16) | copy-start | bytes 147460
  3.4 0.9 copy-start.4
  3.4 0.9 copy-start.5
  3.4 1.3 %copy-start.2 = (s32[2,16,128]{2,1,0:T(8,128)S(1)}, s32[2,16,128]{2,1,0:T(8,128)}, u32[]{:S(2)}) copy-start(s32[2,16,128]{2,1,0:T(8,128)} %wall.1) | copy-start | bytes 49156
  4.3 1.0 %copy-start = (bf16[2,16,64,128]{3,2,1,0:T(8,128)(2,1)S(1)}, bf16[2,16,64,128]{3,2,1,0:T(8,128)(2,1)}, u32[]{:S(2)}) copy-start(bf16[2,16,64,128]{3,2,1,0:T(8,128)(2,1)} %feat.1) | copy-start | bytes 1572868
  4.3 1.2 %copy-start.1 = (bf16[2,16,64,128]{3,2,1,0:T(8,128)(2,1)S(1)}, bf16[2,16,64,128]{3,2,1,0:T(8,128)(2,1)}, u32[]{:S(2)}) copy-start(bf16[2,16,64,128]{3,2,1,0:T(8,128)(2,1)} %cot.1) | copy-start | bytes 1572868

commit v3 on v2

--- a/solution.py
+++ b/solution.py
@@ -201,6 +201,7 @@
     kpart,
     ksum,
     kall,
+    shift,
     send,
     recv,
     hsend,
@@ -246,6 +247,11 @@
 
         lax.fori_loop(low, high, step, 0)
 
+    from_z = lax.broadcasted_iota(jnp.int32, (nz, nz), 0)
+    to_z = lax.broadcasted_iota(jnp.int32, (nz, nz), 1)
+    for m, dz in enumerate([dz for dz in range(-RAD, RAD + 1) if dz]):
+        shift[:, m * nz : (m + 1) * nz] = jnp.where(from_z == to_z + dz, 1.0, 0.0).astype(bf16)
+
     barrier = pltpu.get_barrier_semaphore()
     each(
         1,
@@ -284,20 +290,21 @@
             halo_copy(high_plane, halo.at[0], base + 1, me + 1).wait_send()
             halo_copy(low_plane, halo.at[1], base, me + 1).wait_recv()
 
-    lane = lax.broadcasted_iota(jnp.int32, (ch, nz), 1)
+    moves = [dz for dz in range(-RAD, RAD + 1) if dz]
+    group = math.gcd(ny, 8)
 
     def spread(load, place):
-        def body(y):
-            v = load(y)
-            zs[RAD, place, y + RAD] = v
-            wide = v.astype(f32)
-            for dz in range(-RAD, RAD + 1):
-                if dz:
-                    moved = pltpu.roll(wide, (-dz) % nz, 1)
-                    inside = lane < nz - dz if dz > 0 else lane >= -dz
-                    zs[RAD + dz, place, y + RAD] = jnp.where(inside, moved, 0.0).astype(bf16)
-
-        each(0, ny, body)
+        def body(i):
+            y = i * group
+            v = load(pl.ds(y, group))
+            zs[RAD, place, pl.ds(y + RAD, group)] = v
+            flat = v.reshape(group * ch, nz)
+            moved = jnp.dot(flat, shift[...], preferred_element_type=f32).astype(bf16)
+            for m, dz in enumerate(moves):
+                piece = moved[:, m * nz : (m + 1) * nz].reshape(group, ch, nz)
+                zs[RAD + dz, place, pl.ds(y + RAD, group)] = piece
+
+        each(0, ny // group, body)
 
     def gather_rows(direction):
         def body(y):
@@ -321,11 +328,20 @@
 
         each(0, ny, body)
 
+    unroll = math.gcd(ny, 4)
+
+    def each_row(body):
+        def rows_at(i):
+            for r in range(unroll):
+                body(i * unroll + r)
+
+        each(0, ny // unroll, rows_at)
+
     def mix(weights):
         def body(y):
             local[y] = jnp.dot(weights[...], cat[y], preferred_element_type=f32)
 
-        each(0, ny, body)
+        each_row(body)
 
     def gain(planes, src):
         wide = [p.astype(f32) for p in planes]
@@ -348,7 +364,11 @@
                 total = total + basis[k, peer * xl + j] * vh[k]
             stage[peer, j] = total.astype(bf16)
 
-    each(1, count, lambda d: remote(feat.at[:, ahead(d)], pen1.at[me], 0, d, ahead(d)).start())
+    def each_peer(body):
+        half = count // 2
+        each(1, count, lambda i: body(half + (i // 2) * (1 - 2 * lax.rem(i, 2))))
+
+    each_peer(lambda d: remote(feat.at[:, ahead(d)], pen1.at[me], 0, d, ahead(d)).start())
     low1, high1 = feat.at[0], feat.at[xl - 1]
     halo_start(low1, high1, halo1, 0)
 
@@ -360,26 +380,26 @@
         spread(lambda y: feat[x, y], x + 1)
     acc[...] = jnp.zeros(acc.shape, f32)
     gain([feat[j, me] for j in range(xl)], me)
+
+    def take1(d):
+        src = behind(d)
+        remote(feat.at[:, src], pen1.at[src], 0, d, src).wait_recv()
+        gain([pen1[src, j] for j in range(xl)], src)
+
+    each_peer(take1)
+    channel_mix(wm)
+
+    def give1(d):
+        peer = ahead(d)
+        expand(stage1, peer)
+        remote(stage1.at[peer], spec1.at[me], 1, d, peer).start()
+
+    each_peer(give1)
+    expand(stage1, me)
     halo_wait(low1, high1, halo1, 0)
     spread(lambda y: halo1[0, y], 0)
     spread(lambda y: halo1[1, y], xl + 1)
     gather_rows(1)
-
-    def take1(d):
-        src = behind(d)
-        remote(feat.at[:, src], pen1.at[src], 0, d, src).wait_recv()
-        gain([pen1[src, j] for j in range(xl)], src)
-
-    each(1, count, take1)
-    channel_mix(wm)
-
-    def give1(d):
-        peer = ahead(d)
-        expand(stage1, peer)
-        remote(stage1.at[peer], spec1.at[me], 1, d, peer).start()
-
-    each(1, count, give1)
-    expand(stage1, me)
     mix(wf)
     root = math.sqrt(2.0 / math.pi)
 
@@ -399,12 +419,12 @@
         src = behind(d)
         remote(stage1.at[src], spec1.at[src], 1, d, src).wait_recv()
         slope(src, [spec1[src, j] for j in range(xl)])
-        remote(wgt.at[src], pen2.at[me], 2, count - d, src).start()
-
-    each(1, count, turn)
+
+    each_peer(turn)
 
     low2, high2 = wgt.at[:, 0], wgt.at[:, xl - 1]
     halo_start(low2, high2, halo2, 2)
+    each_peer(lambda d: remote(wgt.at[ahead(d)], pen2.at[me], 2, d, ahead(d)).start())
     for x in range(xl):
         spread(lambda y: wgt[y, x], x + 1)
     acc[...] = jnp.zeros(acc.shape, f32)
@@ -414,13 +434,33 @@
     spread(lambda y: halo2[1, y], xl + 1)
     gather_rows(-1)
 
-    def take2(i):
-        d = count - i
+    kacc[...] = jnp.zeros(kacc.shape, f32)
+
+    def tile_grad(y):
+        field = jnp.concatenate([feat[x, y] for x in range(xl)], axis=1)
+        kacc[...] += lax.dot_general(
+            cat[y, 2 * ch :, :], field, (((1,), (1,)), ((), ())), preferred_element_type=f32
+        )
+
+    each_row(tile_grad)
+    rows = kpart.shape[1]
+    for p in range(count):
+        kpart[p] = kacc[p * rows : (p + 1) * rows]
+    each_peer(lambda d: remote(kpart.at[ahead(d)], ksum.at[me], 4, d, ahead(d)).start())
+
+    def take2(d):
         src = behind(d)
         remote(wgt.at[src], pen2.at[src], 2, d, src).wait_recv()
         gain([pen2[src, j] for j in range(xl)], src)
 
-    each(1, count, take2)
+    each_peer(take2)
+    ksum[me] = kpart[me]
+    each_peer(lambda d: remote(kpart.at[0], ksum.at[behind(d)], 4, d, behind(d)).wait_recv())
+    total = ksum[0]
+    for p in range(1, count):
+        total = total + ksum[p]
+    kall[me] = total * (float(count * xl * ny * nz) ** -0.5)
+    each_peer(lambda d: remote(kall.at[me], kall.at[me], 5, d, ahead(d)).start())
     channel_mix(wmt)
 
     def give2(d):
@@ -428,30 +468,10 @@
         expand(stage2, peer)
         remote(stage2.at[peer], spec2.at[me], 3, d, peer).start()
 
-    each(1, count, give2)
+    each_peer(give2)
     expand(stage2, me)
 
-    kacc[...] = jnp.zeros(kacc.shape, f32)
-
-    def tile_grad(y):
-        field = jnp.concatenate([feat[x, y] for x in range(xl)], axis=1)
-        kacc[...] += lax.dot_general(
-            cat[y, 2 * ch :, :], field, (((1,), (1,)), ((), ())), preferred_element_type=f32
-        )
-
-    each(0, ny, tile_grad)
-    rows = kpart.shape[1]
-    for p in range(count):
-        kpart[p] = kacc[p * rows : (p + 1) * rows]
-    each(1, count, lambda d: remote(kpart.at[ahead(d)], ksum.at[me], 4, d, ahead(d)).start())
     mix(wb)
-    ksum[me] = kpart[me]
-    each(1, count, lambda d: remote(kpart.at[0], ksum.at[behind(d)], 4, d, behind(d)).wait_recv())
-    total = ksum[0]
-    for p in range(1, count):
-        total = total + ksum[p]
-    kall[me] = total * (float(count * xl * ny * nz) ** -0.5)
-    each(1, count, lambda d: remote(kall.at[me], kall.at[me], 5, d, ahead(d)).start())
 
     def finish(y, planes):
         for x in range(xl):
@@ -465,8 +485,8 @@
         remote(stage2.at[src], spec2.at[src], 3, d, src).wait_recv()
         finish(src, [spec2[src, j] for j in range(xl)])
 
-    each(1, count, last)
-    each(1, count, lambda d: remote(kall.at[me], kall.at[behind(d)], 5, d, behind(d)).wait_recv())
+    each_peer(last)
+    each_peer(lambda d: remote(kall.at[me], kall.at[behind(d)], 5, d, behind(d)).wait_recv())
     kout[...] = kall[...]
 
     def drain(d):
@@ -478,7 +498,7 @@
         remote(kpart.at[peer], ksum.at[me], 4, d, peer).wait_send()
         remote(kall.at[me], kall.at[me], 5, d, peer).wait_send()
 
-    each(1, count, drain)
+    each_peer(drain)
 
 
 def fits_kernel(count, features, kernel_weight):
@@ -554,6 +574,7 @@
             pltpu.VMEM((count, rows, ch), f32),
             pltpu.VMEM((count, rows, ch), f32),
             pltpu.VMEM((count, rows, ch), f32),
+            pltpu.VMEM((nz, 2 * RAD * nz), bf16),
             pltpu.SemaphoreType.DMA((6, count)),
             pltpu.SemaphoreType.DMA((6, count)),
             pltpu.SemaphoreType.DMA((4,)),

time: 90 us -> 80.3 us (0.89)
  Pallas kernels: 82.2 us -> 73.1 us
    pallas_call x1, Pallas kernels: 82.2 us -> 73.1 us  [fused_device(): pl.pallas_call(functools.partial(fused_kernel, count), out_shape=(jax.Sha...]
where the time goes in v3:
time: 80.3 us; the launch traced here: 80.1 us
  Pallas kernels  73.1 us (91%)
  local copies, waits for them, and re-layouts  5.95 us (7%)
    pallas_call x1, Pallas kernels, fused_device(): pl.pallas_call(functools.partial(fused_kernel, count), out_shape=(jax.Sha...  73.1 us
    unnamed x22, local copies, waits for them, and re-layouts  5.38 us

profile of v3, /device:TPU:0, one launch (start us, length us, event | category | flops | bytes accessed | tf_op | source)
XLA Modules:
  0.0 80.1 jit_solution(2025931225832189452)
XLA Ops:
  0.7 0.0 copy-start.8
  0.7 0.0 copy-start.6
  0.7 0.6 copy-done.8
  1.3 0.0 copy-done.6
  1.4 0.1 copy.15.offs
  1.4 0.0 copy-start.7
  1.5 0.1 fusion.basis
  1.6 0.5 copy-done.7
  2.1 0.1 broadcast_in_dim.42.bias
  2.2 1.1 %copy.14 = bf16[16,64,64]{1,2,0:T(8,128)(2,1)S(1)} copy(bf16[16,64,64]{2,1,0:T(8,128)(2,1)} %param.18) | data formatting | bytes 262144 | tf_op args[8]
  3.4 0.0 copy-start.3
  3.4 0.0 copy-start.4
  3.4 0.0 copy-start.5
  3.4 0.0 copy-start.2
  3.4 0.2 copy.16.wm
  3.6 0.7 copy-done.3
  4.3 0.0 copy-done.4
  4.3 0.0 copy-done.5
  4.3 0.0 copy-start
  4.3 0.0 copy-start.1
  4.3 0.1 copy.17.wb
  4.4 0.1 copy.12
  4.5 0.1 reshape.51.wf
  4.7 0.0 copy-done.2
  4.7 0.6 copy-done
  5.3 0.2 copy-done.1
  5.5 73.1 %shard_map.113 = (bf16[2,16,64,128]{3,2,1,0:T(8,128)(2,1)S(1)}, f32[16,24,64]{2,1,0:T(8,128)S(1)}) custom-call(bf16[2,16,64,128]{3,2,1,0:T(8,128)(2,1)S(1)} %copy-done, bf16[2,16,64,128]{3,2,1,0:T(8,128)(2,1)S(1)} %copy-done.1, s32[2,16,128]{2,1,0:T(8,128)S(1)} %copy-done.2, s32[6,3]{1,0:T(8,128)S(1)} %copy.15.offs, f32[16,32]{1,0:T(8,128)S(1)} %fusion.basis, ...), custom_call_target="tpu_custom_call" | custom-call | tf_op jit(solution)/shard_map/pallas_call | solution.py:550
  78.6 0.8 copy.20
  79.4 0.7 copy.21
  (6 shorter events, 0.1 us)
Async XLA Ops:
  0.7 0.7 copy-start.8
  0.7 0.7 copy-start.6
  1.4 0.7 copy-start.7
  3.4 0.9 %copy-start.3 = (bf16[6,64,64]{2,1,0:T(8,128)(2,1)S(1)}, bf16[6,64,64]{2,1,0:T(8,128)(2,1)}, u32[]{:S(2)}) copy-start(bf16[6,64,64]{2,1,0:T(8,128)(2,1)} %param.16) | copy-start | bytes 147460
  3.4 0.9 %copy-start.4 = (bf16[64,64]{1,0:T(8,128)(2,1)S(1)}, bf16[64,64]{1,0:T(8,128)(2,1)}, u32[]{:S(2)}) copy-start(bf16[64,64]{1,0:T(8,128)(2,1)} %param.17) | copy-start | bytes 24580
  3.4 0.9 %copy-start.5 = (bf16[64,64]{1,0:T(8,128)(2,1)S(1)}, bf16[64,64]{1,0:T(8,128)(2,1)}, u32[]{:S(2)}) copy-start(bf16[64,64]{1,0:T(8,128)(2,1)} %param.15) | copy-start | bytes 24580
  3.4 1.3 %copy-start.2 = (s32[2,16,128]{2,1,0:T(8,128)S(1)}, s32[2,16,128]{2,1,0:T(8,128)}, u32[]{:S(2)}) copy-start(s32[2,16,128]{2,1,0:T(8,128)} %wall.1) | copy-start | bytes 49156
  4.3 1.0 %copy-start = (bf16[2,16,64,128]{3,2,1,0:T(8,128)(2,1)S(1)}, bf16[2,16,64,128]{3,2,1,0:T(8,128)(2,1)}, u32[]{:S(2)}) copy-start(bf16[2,16,64,128]{3,2,1,0:T(8,128)(2,1)} %feat.1) | copy-start | bytes 1572868
  4.3 1.2 %copy-start.1 = (bf16[2,16,64,128]{3,2,1,0:T(8,128)(2,1)S(1)}, bf16[2,16,64,128]{3,2,1,0:T(8,128)(2,1)}, u32[]{:S(2)}) copy-start(bf16[2,16,64,128]{3,2,1,0:T(8,128)(2,1)} %cot.1) | copy-start | bytes 1572868

commit v4 on v3

--- a/solution.py
+++ b/solution.py
@@ -454,6 +454,15 @@
         gain([pen2[src, j] for j in range(xl)], src)
 
     each_peer(take2)
+    channel_mix(wmt)
+
+    def give2(d):
+        peer = ahead(d)
+        expand(stage2, peer)
+        remote(stage2.at[peer], spec2.at[me], 3, d, peer).start()
+
+    each_peer(give2)
+    expand(stage2, me)
     ksum[me] = kpart[me]
     each_peer(lambda d: remote(kpart.at[0], ksum.at[behind(d)], 4, d, behind(d)).wait_recv())
     total = ksum[0]
@@ -461,15 +470,6 @@
         total = total + ksum[p]
     kall[me] = total * (float(count * xl * ny * nz) ** -0.5)
     each_peer(lambda d: remote(kall.at[me], kall.at[me], 5, d, ahead(d)).start())
-    channel_mix(wmt)
-
-    def give2(d):
-        peer = ahead(d)
-        expand(stage2, peer)
-        remote(stage2.at[peer], spec2.at[me], 3, d, peer).start()
-
-    each_peer(give2)
-    expand(stage2, me)
 
     mix(wb)
 

time: 80.3 us -> 77.7 us (0.968)
  Pallas kernels: 73.1 us -> 70.5 us
    pallas_call x1, Pallas kernels: 73.1 us -> 70.5 us  [fused_device(): pl.pallas_call(functools.partial(fused_kernel, count), out_shape=(jax.Sha...]
where the time goes in v4:
time: 77.7 us; the launch traced here: 77.5 us
  Pallas kernels  70.5 us (91%)
  local copies, waits for them, and re-layouts  5.95 us (8%)
    pallas_call x1, Pallas kernels, fused_device(): pl.pallas_call(functools.partial(fused_kernel, count), out_shape=(jax.Sha...  70.5 us
    unnamed x22, local copies, waits for them, and re-layouts  5.38 us

profile of v4, /device:TPU:0, one launch (start us, length us, event | category | flops | bytes accessed | tf_op | source)
XLA Modules:
  0.0 77.5 jit_solution(10655895810564171323)
XLA Ops:
  0.7 0.0 copy-start.8
  0.7 0.0 copy-start.6
  0.7 0.6 copy-done.8
  1.3 0.0 copy-done.6
  1.4 0.1 copy.15.offs
  1.4 0.0 copy-start.7
  1.5 0.1 fusion.basis
  1.6 0.5 copy-done.7
  2.1 0.1 broadcast_in_dim.42.bias
  2.2 1.1 %copy.14 = bf16[16,64,64]{1,2,0:T(8,128)(2,1)S(1)} copy(bf16[16,64,64]{2,1,0:T(8,128)(2,1)} %param.18) | data formatting | bytes 262144 | tf_op args[8]
  3.4 0.0 copy-start.3
  3.4 0.0 copy-start.4
  3.4 0.0 copy-start.5
  3.4 0.0 copy-start.2
  3.4 0.2 copy.16.wm
  3.6 0.7 copy-done.3
  4.3 0.0 copy-done.4
  4.3 0.0 copy-done.5
  4.3 0.0 copy-start
  4.3 0.0 copy-start.1
  4.3 0.1 copy.17.wb
  4.4 0.1 copy.12
  4.5 0.1 reshape.51.wf
  4.7 0.0 copy-done.2
  4.7 0.6 copy-done
  5.3 0.2 copy-done.1
  5.5 70.5 %shard_map.113 = (bf16[2,16,64,128]{3,2,1,0:T(8,128)(2,1)S(1)}, f32[16,24,64]{2,1,0:T(8,128)S(1)}) custom-call(bf16[2,16,64,128]{3,2,1,0:T(8,128)(2,1)S(1)} %copy-done, bf16[2,16,64,128]{3,2,1,0:T(8,128)(2,1)S(1)} %copy-done.1, s32[2,16,128]{2,1,0:T(8,128)S(1)} %copy-done.2, s32[6,3]{1,0:T(8,128)S(1)} %copy.15.offs, f32[16,32]{1,0:T(8,128)S(1)} %fusion.basis, ...), custom_call_target="tpu_custom_call" | custom-call | tf_op jit(solution)/shard_map/pallas_call | solution.py:550
  76.0 0.8 %copy.20 = bf16[2,16,64,128]{3,2,1,0:T(8,128)(2,1)} copy(bf16[2,16,64,128]{3,2,1,0:T(8,128)(2,1)S(1)} %get-tuple-element.12) | data formatting | bytes 1048576
  76.8 0.7 copy.21
  (6 shorter events, 0.1 us)
Async XLA Ops:
  0.7 0.7 copy-start.8
  0.7 0.7 copy-start.6
  1.4 0.7 copy-start.7
  3.4 0.9 %copy-start.3 = (bf16[6,64,64]{2,1,0:T(8,128)(2,1)S(1)}, bf16[6,64,64]{2,1,0:T(8,128)(2,1)}, u32[]{:S(2)}) copy-start(bf16[6,64,64]{2,1,0:T(8,128)(2,1)} %param.16) | copy-start | bytes 147460
  3.4 0.9 %copy-start.4 = (bf16[64,64]{1,0:T(8,128)(2,1)S(1)}, bf16[64,64]{1,0:T(8,128)(2,1)}, u32[]{:S(2)}) copy-start(bf16[64,64]{1,0:T(8,128)(2,1)} %param.17) | copy-start | bytes 24580
  3.4 0.9 %copy-start.5 = (bf16[64,64]{1,0:T(8,128)(2,1)S(1)}, bf16[64,64]{1,0:T(8,128)(2,1)}, u32[]{:S(2)}) copy-start(bf16[64,64]{1,0:T(8,128)(2,1)} %param.15) | copy-start | bytes 24580
  3.4 1.3 %copy-start.2 = (s32[2,16,128]{2,1,0:T(8,128)S(1)}, s32[2,16,128]{2,1,0:T(8,128)}, u32[]{:S(2)}) copy-start(s32[2,16,128]{2,1,0:T(8,128)} %wall.1) | copy-start | bytes 49156
  4.3 1.0 %copy-start = (bf16[2,16,64,128]{3,2,1,0:T(8,128)(2,1)S(1)}, bf16[2,16,64,128]{3,2,1,0:T(8,128)(2,1)}, u32[]{:S(2)}) copy-start(bf16[2,16,64,128]{3,2,1,0:T(8,128)(2,1)} %feat.1) | copy-start | bytes 1572868
  4.3 1.2 %copy-start.1 = (bf16[2,16,64,128]{3,2,1,0:T(8,128)(2,1)S(1)}, bf16[2,16,64,128]{3,2,1,0:T(8,128)(2,1)}, u32[]{:S(2)}) copy-start(bf16[2,16,64,128]{3,2,1,0:T(8,128)(2,1)} %cot.1) | copy-start | bytes 1572868
